TPU v7x, 32 devices: a whole 2x2x4 slice. The times are simulated.
32 devices in a mesh: rep: 4 (over z), shard: 8 (over y, x, core).
Axes of the slice: x: 2, y: 2, z: 4, core: 2. Of those that a mesh axis runs over, the one named last changes fastest.
Arguments:
- stream_input: bfloat16 [64, 96, 1024], P(('rep', 'shard')), may hold values from -6 to 6
- output_cotangent: bfloat16 [64, 96, 1024], P(('rep', 'shard')), may hold values from -6 to 6
- image_mask: int32 [64], P(('rep', 'shard')), may hold values 0 or 1
- first_gain: bfloat16 [2, 1024], P(None, 'shard'), may hold values from 0.5 to 1.5
- first_shift: bfloat16 [2, 1024], P(None, 'shard'), may hold values from -0.59765625 to 0.59765625
- query_matrix: bfloat16 [2, 1024, 1024], P(None, 'shard'), may hold values from -0.25 to 0.25
- query_offset: bfloat16 [2, 1024], P(None, 'shard'), may hold values from -0.59765625 to 0.59765625
- key_matrix: bfloat16 [2, 1024, 1024], P(None, 'shard'), may hold values from -0.1875 to 0.1875
- value_matrix: bfloat16 [2, 1024, 1024], P(None, 'shard'), may hold values from -0.1875 to 0.1875
- value_offset: bfloat16 [2, 1024], P(None, 'shard'), may hold values from -0.59765625 to 0.59765625
- out_matrix: bfloat16 [2, 1024, 1024], P(None, 'shard'), may hold values from -0.75 to 0.75
- out_offset: bfloat16 [2, 1024], P(None, 'shard'), may hold values from -0.59765625 to 0.59765625
- second_gain: bfloat16 [2, 1024], P(None, 'shard'), may hold values from 0.5 to 1.5
- second_shift: bfloat16 [2, 1024], P(None, 'shard'), may hold values from -0.59765625 to 0.59765625
- expand_matrix: bfloat16 [2, 1024, 4096], P(None, 'shard'), may hold values from -0.1875 to 0.1875
- expand_offset: bfloat16 [2, 4096], P(None, 'shard'), may hold values from -0.59765625 to 0.59765625
- reduce_matrix: bfloat16 [2, 4096, 1024], P(None, 'shard'), may hold values from -0.125 to 0.125
- reduce_offset: bfloat16 [2, 1024], P(None, 'shard'), may hold values from -0.59765625 to 0.59765625
Outputs:
- stream_output: bfloat16 [64, 96, 1024], P(('rep', 'shard'))
- input_grad: float32 [64, 96, 1024], P(('rep', 'shard'))
- grad_first_gain: float32 [2, 1024], P(None, 'shard')
- grad_first_shift: float32 [2, 1024], P(None, 'shard')
- grad_query_matrix: float32 [2, 1024, 1024], P(None, 'shard')
- grad_query_offset: float32 [2, 1024], P(None, 'shard')
- grad_key_matrix: float32 [2, 1024, 1024], P(None, 'shard')
- grad_value_matrix: float32 [2, 1024, 1024], P(None, 'shard')
- grad_value_offset: float32 [2, 1024], P(None, 'shard')
- grad_out_matrix: float32 [2, 1024, 1024], P(None, 'shard')
- grad_out_offset: float32 [2, 1024], P(None, 'shard')
- grad_second_gain: float32 [2, 1024], P(None, 'shard')
- grad_second_shift: float32 [2, 1024], P(None, 'shard')
- grad_expand_matrix: float32 [2, 1024, 4096], P(None, 'shard')
- grad_expand_offset: float32 [2, 4096], P(None, 'shard')
- grad_reduce_matrix: float32 [2, 4096, 1024], P(None, 'shard')
- grad_reduce_offset: float32 [2, 1024], P(None, 'shard')
Inputs may be any that keep to these rules, and one draw needn't show every extreme that they name: image_mask holds only 0 and 1.
All inputs are finite; a program needn't handle non-finite values. No bound on the sum of `image_mask` on one device may be relied on, other than what follows from the above.
Results may differ from a plain program's by a relative error of at most 0.025.
Values may be sent and summed in bfloat16 or wider, within the bound.
No kernel may reach another device: no remote copies, remote signals or barrier semaphores. Data moves between devices by JAX's collectives and lax.ppermute only.
A program may use at most 320 MiB of HBM per device.

v0:
```python
import jax
import jax.numpy as jnp
from jax import lax
from jax.sharding import PartitionSpec as P

HEADS = 16
HEAD_DIM = 64
LAYERS = 2
MICRO = 2


epsilon = 1e-05


def product(left, right):
    return jnp.dot(left, right, preferred_element_type=jnp.float32)


def product_left(left, right):
    return lax.dot_general(
        left, right, (((0,), (0,)), ((), ())), preferred_element_type=jnp.float32
    )


def product_right(left, right):
    return lax.dot_general(
        left, right, (((1,), (1,)), ((), ())), preferred_element_type=jnp.float32
    )


def split_heads(values):
    return values.reshape(MICRO, -1, HEADS, HEAD_DIM)


def column_sum(values):
    return jnp.sum(values.astype(jnp.float32), axis=0)


def normalize(values, gain, shift):
    center = values - jnp.mean(values, axis=-1, keepdims=True)
    spread = jnp.mean(center * center, axis=-1, keepdims=True)
    inverse = lax.rsqrt(spread + epsilon)
    scaled = center * inverse
    return (scaled * gain + shift, scaled, inverse)


def norm_back(upstream, scaled, inverse, gain):
    slope = upstream * gain
    inner = (
        slope
        - jnp.mean(slope, axis=-1, keepdims=True)
        - scaled * jnp.mean(slope * scaled, axis=-1, keepdims=True)
    )
    return (inner * inverse, jnp.sum(upstream * scaled, axis=0), jnp.sum(upstream, axis=0))


def layer_forward(stream, weights):
    (
        gain_one,
        shift_one,
        query_matrix,
        query_offset,
        key_matrix,
        value_matrix,
        value_offset,
        out_matrix,
        out_offset,
        gain_two,
        shift_two,
        expand_matrix,
        expand_offset,
        reduce_matrix,
        reduce_offset,
    ) = weights
    width = stream.shape[1]
    factor = HEAD_DIM ** (-0.5)
    normed, scaled_one, inverse_one = normalize(
        stream, gain_one.astype(jnp.float32), shift_one.astype(jnp.float32)
    )
    normed_low = normed.astype(jnp.bfloat16)
    queries = (product(normed_low, query_matrix) + query_offset.astype(jnp.float32)).astype(
        jnp.bfloat16
    )
    keys = product(normed_low, key_matrix).astype(jnp.bfloat16)
    values = (product(normed_low, value_matrix) + value_offset.astype(jnp.float32)).astype(
        jnp.bfloat16
    )
    scores = (
        jnp.einsum(
            "bqhd,bkhd->bhqk",
            split_heads(queries),
            split_heads(keys),
            preferred_element_type=jnp.float32,
        )
        * factor
    )
    top = jnp.max(scores, axis=-1, keepdims=True)
    raised = jnp.exp(scores - top)
    total = jnp.sum(raised, axis=-1, keepdims=True)
    probs = raised / total
    logsum = top + jnp.log(total)
    mixed = jnp.einsum(
        "bhqk,bkhd->bqhd",
        probs.astype(jnp.bfloat16),
        split_heads(values),
        preferred_element_type=jnp.float32,
    )
    mixed_low = mixed.reshape(-1, width).astype(jnp.bfloat16)
    middle = stream + (product(mixed_low, out_matrix) + out_offset.astype(jnp.float32))
    normed_two, scaled_two, inverse_two = normalize(
        middle, gain_two.astype(jnp.float32), shift_two.astype(jnp.float32)
    )
    normed_two_low = normed_two.astype(jnp.bfloat16)
    hidden = product(normed_two_low, expand_matrix) + expand_offset.astype(jnp.float32)
    active = (hidden * jax.nn.sigmoid(1.702 * hidden)).astype(jnp.bfloat16)
    result = middle + (product(active, reduce_matrix) + reduce_offset.astype(jnp.float32))
    kept = (
        scaled_one,
        inverse_one,
        normed_low,
        queries,
        keys,
        values,
        logsum,
        mixed_low,
        scaled_two,
        inverse_two,
        normed_two_low,
        hidden,
        active,
    )
    return (result, kept)


def layer_backward(upstream, kept, weights):
    (
        gain_one,
        shift_one,
        query_matrix,
        query_offset,
        key_matrix,
        value_matrix,
        value_offset,
        out_matrix,
        out_offset,
        gain_two,
        shift_two,
        expand_matrix,
        expand_offset,
        reduce_matrix,
        reduce_offset,
    ) = weights
    (
        scaled_one,
        inverse_one,
        normed_low,
        queries,
        keys,
        values,
        logsum,
        mixed_low,
        scaled_two,
        inverse_two,
        normed_two_low,
        hidden,
        active,
    ) = kept
    width = upstream.shape[1]
    factor = HEAD_DIM ** (-0.5)
    branch = upstream.astype(jnp.bfloat16)
    reduce_grad = product_left(active, branch)
    reduce_bias_grad = column_sum(branch)
    back_active = product_right(branch, reduce_matrix)
    sigma = jax.nn.sigmoid(1.702 * hidden)
    back_hidden = (back_active * (sigma + 1.702 * hidden * sigma * (1.0 - sigma))).astype(
        jnp.bfloat16
    )
    expand_grad = product_left(normed_two_low, back_hidden)
    expand_bias_grad = column_sum(back_hidden)
    back_normed_two = product_right(back_hidden, expand_matrix)
    back_norm_two, gain_two_grad, shift_two_grad = norm_back(
        back_normed_two, scaled_two, inverse_two, gain_two.astype(jnp.float32)
    )
    back_middle = upstream + back_norm_two
    branch_two = back_middle.astype(jnp.bfloat16)
    out_grad = product_left(mixed_low, branch_two)
    out_bias_grad = column_sum(branch_two)
    back_mixed = split_heads(product_right(branch_two, out_matrix).astype(jnp.bfloat16))
    scores = (
        jnp.einsum(
            "bqhd,bkhd->bhqk",
            split_heads(queries),
            split_heads(keys),
            preferred_element_type=jnp.float32,
        )
        * factor
    )
    probs = jnp.exp(scores - logsum)
    back_probs = jnp.einsum(
        "bqhd,bkhd->bhqk", back_mixed, split_heads(values), preferred_element_type=jnp.float32
    )
    delta = jnp.sum(probs * back_probs, axis=-1, keepdims=True)
    back_scores = (probs * (back_probs - delta)).astype(jnp.bfloat16)
    back_values = jnp.einsum(
        "bhqk,bqhd->bkhd",
        probs.astype(jnp.bfloat16),
        back_mixed,
        preferred_element_type=jnp.float32,
    )
    back_values = back_values.reshape(-1, width).astype(jnp.bfloat16)
    back_queries = (
        jnp.einsum(
            "bhqk,bkhd->bqhd", back_scores, split_heads(keys), preferred_element_type=jnp.float32
        )
        * factor
    )
    back_queries = back_queries.reshape(-1, width).astype(jnp.bfloat16)
    back_keys = (
        jnp.einsum(
            "bhqk,bqhd->bkhd", back_scores, split_heads(queries), preferred_element_type=jnp.float32
        )
        * factor
    )
    back_keys = back_keys.reshape(-1, width).astype(jnp.bfloat16)
    query_grad = product_left(normed_low, back_queries)
    query_bias_grad = column_sum(back_queries)
    key_grad = product_left(normed_low, back_keys)
    value_grad = product_left(normed_low, back_values)
    value_bias_grad = column_sum(back_values)
    back_normed = (
        product_right(back_queries, query_matrix)
        + product_right(back_keys, key_matrix)
        + product_right(back_values, value_matrix)
    )
    back_norm_one, gain_one_grad, shift_one_grad = norm_back(
        back_normed, scaled_one, inverse_one, gain_one.astype(jnp.float32)
    )
    grads = (
        gain_one_grad,
        shift_one_grad,
        query_grad,
        query_bias_grad,
        key_grad,
        value_grad,
        value_bias_grad,
        out_grad,
        out_bias_grad,
        gain_two_grad,
        shift_two_grad,
        expand_grad,
        expand_bias_grad,
        reduce_grad,
        reduce_bias_grad,
    )
    return (back_middle + back_norm_one, grads)


def fetch_forward(params, layer):
    parts = [piece[layer] for piece in params]
    return (
        lax.all_gather(parts[0], "shard", axis=0, tiled=True),
        lax.all_gather(parts[1], "shard", axis=0, tiled=True),
        lax.all_gather(parts[2], "shard", axis=0, tiled=True),
        lax.all_gather(parts[3], "shard", axis=0, tiled=True),
        lax.all_gather(parts[4], "shard", axis=0, tiled=True),
        lax.all_gather(parts[5], "shard", axis=0, tiled=True),
        lax.all_gather(parts[6], "shard", axis=0, tiled=True),
        lax.all_gather(parts[7], "shard", axis=0, tiled=True),
        lax.all_gather(parts[8], "shard", axis=0, tiled=True),
        lax.all_gather(parts[9], "shard", axis=0, tiled=True),
        lax.all_gather(parts[10], "shard", axis=0, tiled=True),
        lax.all_gather(parts[11], "shard", axis=0, tiled=True),
        lax.all_gather(parts[12], "shard", axis=0, tiled=True),
        lax.all_gather(parts[13], "shard", axis=0, tiled=True),
        lax.all_gather(parts[14], "shard", axis=0, tiled=True),
    )


def fetch_backward(params, layer):
    parts = [piece[layer] for piece in params]
    return (
        lax.all_gather(parts[0], "shard", axis=0, tiled=True),
        lax.all_gather(parts[1], "shard", axis=0, tiled=True),
        lax.all_gather(parts[2], "shard", axis=0, tiled=True),
        lax.all_gather(parts[3], "shard", axis=0, tiled=True),
        lax.all_gather(parts[4], "shard", axis=0, tiled=True),
        lax.all_gather(parts[5], "shard", axis=0, tiled=True),
        lax.all_gather(parts[6], "shard", axis=0, tiled=True),
        lax.all_gather(parts[7], "shard", axis=0, tiled=True),
        lax.all_gather(parts[8], "shard", axis=0, tiled=True),
        lax.all_gather(parts[9], "shard", axis=0, tiled=True),
        lax.all_gather(parts[10], "shard", axis=0, tiled=True),
        lax.all_gather(parts[11], "shard", axis=0, tiled=True),
        lax.all_gather(parts[12], "shard", axis=0, tiled=True),
        lax.all_gather(parts[13], "shard", axis=0, tiled=True),
        lax.all_gather(parts[14], "shard", axis=0, tiled=True),
    )


def owner_part(grads):
    return (
        lax.psum_scatter(grads[0], "shard", scatter_dimension=0, tiled=True),
        lax.psum_scatter(grads[1], "shard", scatter_dimension=0, tiled=True),
        lax.psum_scatter(grads[2], "shard", scatter_dimension=0, tiled=True),
        lax.psum_scatter(grads[3], "shard", scatter_dimension=0, tiled=True),
        lax.psum_scatter(grads[4], "shard", scatter_dimension=0, tiled=True),
        lax.psum_scatter(grads[5], "shard", scatter_dimension=0, tiled=True),
        lax.psum_scatter(grads[6], "shard", scatter_dimension=0, tiled=True),
        lax.psum_scatter(grads[7], "shard", scatter_dimension=0, tiled=True),
        lax.psum_scatter(grads[8], "shard", scatter_dimension=0, tiled=True),
        lax.psum_scatter(grads[9], "shard", scatter_dimension=0, tiled=True),
        lax.psum_scatter(grads[10], "shard", scatter_dimension=0, tiled=True),
        lax.psum_scatter(grads[11], "shard", scatter_dimension=0, tiled=True),
        lax.psum_scatter(grads[12], "shard", scatter_dimension=0, tiled=True),
        lax.psum_scatter(grads[13], "shard", scatter_dimension=0, tiled=True),
        lax.psum_scatter(grads[14], "shard", scatter_dimension=0, tiled=True),
    )


def shards(
    stream_input,
    output_cotangent,
    image_mask,
    first_gain,
    first_shift,
    query_matrix,
    query_offset,
    key_matrix,
    value_matrix,
    value_offset,
    out_matrix,
    out_offset,
    second_gain,
    second_shift,
    expand_matrix,
    expand_offset,
    reduce_matrix,
    reduce_offset,
):
    params = (
        first_gain,
        first_shift,
        query_matrix,
        query_offset,
        key_matrix,
        value_matrix,
        value_offset,
        out_matrix,
        out_offset,
        second_gain,
        second_shift,
        expand_matrix,
        expand_offset,
        reduce_matrix,
        reduce_offset,
    )
    images = stream_input.shape[0]
    length = stream_input.shape[1]
    width = stream_input.shape[2]
    maskf = image_mask.astype(jnp.float32)[:, None, None]
    stream = stream_input.astype(jnp.float32).reshape(images * length, width)
    saved = []
    for layer in range(LAYERS):
        stream, kept = layer_forward(stream, fetch_forward(params, layer))
        saved.append(kept)
    output = (stream.reshape(images, length, width) * maskf).astype(jnp.bfloat16)
    upstream = (output_cotangent.astype(jnp.float32) * maskf).reshape(images * length, width)
    owned = [None] * LAYERS
    for layer in reversed(range(LAYERS)):
        upstream, grads = layer_backward(upstream, saved[layer], fetch_backward(params, layer))
        owned[layer] = owner_part(grads)
    stacked = [jnp.stack([owned[layer][index] for layer in range(LAYERS)]) for index in range(15)]
    summed = (
        lax.psum(stacked[0].astype(jnp.bfloat16), "rep").astype(jnp.float32),
        lax.psum(stacked[1].astype(jnp.bfloat16), "rep").astype(jnp.float32),
        lax.psum(stacked[2].astype(jnp.bfloat16), "rep").astype(jnp.float32),
        lax.psum(stacked[3].astype(jnp.bfloat16), "rep").astype(jnp.float32),
        lax.psum(stacked[4].astype(jnp.bfloat16), "rep").astype(jnp.float32),
        lax.psum(stacked[5].astype(jnp.bfloat16), "rep").astype(jnp.float32),
        lax.psum(stacked[6].astype(jnp.bfloat16), "rep").astype(jnp.float32),
        lax.psum(stacked[7].astype(jnp.bfloat16), "rep").astype(jnp.float32),
        lax.psum(stacked[8].astype(jnp.bfloat16), "rep").astype(jnp.float32),
        lax.psum(stacked[9].astype(jnp.bfloat16), "rep").astype(jnp.float32),
        lax.psum(stacked[10].astype(jnp.bfloat16), "rep").astype(jnp.float32),
        lax.psum(stacked[11].astype(jnp.bfloat16), "rep").astype(jnp.float32),
        lax.psum(stacked[12].astype(jnp.bfloat16), "rep").astype(jnp.float32),
        lax.psum(stacked[13].astype(jnp.bfloat16), "rep").astype(jnp.float32),
        lax.psum(stacked[14].astype(jnp.bfloat16), "rep").astype(jnp.float32),
    )
    return (output, upstream.reshape(images, length, width)) + tuple(summed)


def solution(mesh):
    placed = (
        P(("rep", "shard"), None, None),
        P(("rep", "shard"), None, None),
        P(("rep", "shard")),
        P(None, "shard"),
        P(None, "shard"),
        P(None, "shard", None),
        P(None, "shard"),
        P(None, "shard", None),
        P(None, "shard", None),
        P(None, "shard"),
        P(None, "shard", None),
        P(None, "shard"),
        P(None, "shard"),
        P(None, "shard"),
        P(None, "shard", None),
        P(None, "shard"),
        P(None, "shard", None),
        P(None, "shard"),
    )
    return jax.shard_map(
        shards,
        mesh=mesh,
        in_specs=placed,
        out_specs=(
            P(("rep", "shard"), None, None),
            P(("rep", "shard"), None, None),
            P(None, "shard"),
            P(None, "shard"),
            P(None, "shard", None),
            P(None, "shard"),
            P(None, "shard", None),
            P(None, "shard", None),
            P(None, "shard"),
            P(None, "shard", None),
            P(None, "shard"),
            P(None, "shard"),
            P(None, "shard"),
            P(None, "shard", None),
            P(None, "shard"),
            P(None, "shard", None),
            P(None, "shard"),
        ),
        check_vma=False,
    )
```

profile of v0, /device:TPU:0, one launch (start us, length us, event | category | flops | bytes accessed | tf_op | source)
XLA Modules:
  0.0 1673.9 jit_solution(16758169006493100423)
XLA Ops:
  24.2 10.2 all-gather
  205.9 38.8 %all-gather.53.cloned.1.call-done = bf16[1,4096,1024]{2,1,0:T(8,128)(2,1)} async-done(((bf16[1,512,1024]{2,1,0:T(8,128)(2,1)}), bf16[1,4096,1024]{2,1,0:T(8,128)(2,1)}) %all-gather.53.cloned.1.call-update) | async-done | bytes 8388624 | tf_op jit(solution)/shard_map/all_gather | solution.py:274
  252.1 22.9 %all-gather.57.cloned.1.call-done = bf16[1,1024,1024]{2,1,0:T(8,128)(2,1)} async-done(((bf16[1,128,1024]{2,1,0:T(8,128)(2,1)}), bf16[1,1024,1024]{2,1,0:T(8,128)(2,1)}) %all-gather.57.cloned.1.call-update) | async-done | bytes 2097168 | tf_op jit(solution)/shard_map/all_gather | solution.py:263
  279.5 25.3 %all-gather.59.cloned.1.call-done = bf16[1,1024,1024]{2,1,0:T(8,128)(2,1)} async-done(((bf16[1,128,1024]{2,1,0:T(8,128)(2,1)}), bf16[1,1024,1024]{2,1,0:T(8,128)(2,1)}) %all-gather.59.cloned.1.call-update) | async-done | bytes 2097168 | tf_op jit(solution)/shard_map/all_gather | solution.py:265
  308.9 26.3 %all-gather.55.cloned.1.call-done = bf16[1,1024,1024]{2,1,0:T(8,128)(2,1)} async-done(((bf16[1,128,1024]{2,1,0:T(8,128)(2,1)}), bf16[1,1024,1024]{2,1,0:T(8,128)(2,1)}) %all-gather.55.cloned.1.call-update) | async-done | bytes 2097168 | tf_op jit(solution)/shard_map/all_gather | solution.py:266
  345.5 19.4 %all-gather.61.cloned.1.call-done = bf16[1,1024,1024]{2,1,0:T(8,128)(2,1)} async-done(((bf16[1,128,1024]{2,1,0:T(8,128)(2,1)}), bf16[1,1024,1024]{2,1,0:T(8,128)(2,1)}) %all-gather.61.cloned.1.call-update) | async-done | bytes 2097168 | tf_op jit(solution)/shard_map/all_gather | solution.py:268
  368.8 53.0 %all-gather.63.cloned.1.call-done = bf16[1,1024,4096]{2,1,0:T(8,128)(2,1)} async-done(((bf16[1,128,4096]{2,1,0:T(8,128)(2,1)}), bf16[1,1024,4096]{2,1,0:T(8,128)(2,1)}) %all-gather.63.cloned.1.call-update) | async-done | bytes 8388624 | tf_op jit(solution)/shard_map/all_gather | solution.py:272
  428.9 49.6 %all-gather.65.cloned.1.call-done = bf16[1,4096,1024]{2,1,0:T(8,128)(2,1)} async-done(((bf16[1,512,1024]{2,1,0:T(8,128)(2,1)}), bf16[1,4096,1024]{2,1,0:T(8,128)(2,1)}) %all-gather.65.cloned.1.call-update) | async-done | bytes 8388624 | tf_op jit(solution)/shard_map/all_gather | solution.py:274
  606.0 10.2 fusion.175
  617.2 10.2 fusion.183
  628.6 10.3 fusion.182
  652.3 21.4 %reduce-scatter.23.cloned.1.call-done = f32[128,1024]{1,0:T(8,128)} async-done(((f32[1024,1024]{1,0:T(8,128)}), f32[128,1024]{1,0:T(8,128)}) %reduce-scatter.23.cloned.1.call-update) | async-done | bytes 524304 | tf_op jit(solution)/shard_map/reduce_scatter | solution.py:307
  674.8 53.9 %reduce-scatter.21.cloned.1.call-done = f32[128,1024]{1,0:T(8,128)} async-done(((f32[1024,1024]{1,0:T(8,128)}), f32[128,1024]{1,0:T(8,128)}) %reduce-scatter.21.cloned.1.call-update) | async-done | bytes 524304 | tf_op jit(solution)/shard_map/reduce_scatter | solution.py:307
  730.6 52.6 %reduce-scatter.19.cloned.1.call-done = f32[128,1024]{1,0:T(8,128)} async-done(((f32[1024,1024]{1,0:T(8,128)}), f32[128,1024]{1,0:T(8,128)}) %reduce-scatter.19.cloned.1.call-update) | async-done | bytes 524304 | tf_op jit(solution)/shard_map/reduce_scatter | solution.py:306
  784.2 53.9 %reduce-scatter.17.cloned.1.call-done = f32[128,1024]{1,0:T(8,128)} async-done(((f32[1024,1024]{1,0:T(8,128)}), f32[128,1024]{1,0:T(8,128)}) %reduce-scatter.17.cloned.1.call-update) | async-done | bytes 524304 | tf_op jit(solution)/shard_map/reduce_scatter | solution.py:306
  840.1 53.4 %reduce-scatter.15.cloned.1.call-done = f32[128,1024]{1,0:T(8,128)} async-done(((f32[1024,1024]{1,0:T(8,128)}), f32[128,1024]{1,0:T(8,128)}) %reduce-scatter.15.cloned.1.call-update) | async-done | bytes 524304 | tf_op jit(solution)/shard_map/reduce_scatter | solution.py:304
  894.5 54.4 %reduce-scatter.13.cloned.1.call-done = f32[128,1024]{1,0:T(8,128)} async-done(((f32[1024,1024]{1,0:T(8,128)}), f32[128,1024]{1,0:T(8,128)}) %reduce-scatter.13.cloned.1.call-update) | async-done | bytes 524304 | tf_op jit(solution)/shard_map/reduce_scatter | solution.py:304
  950.8 117.6 %reduce-scatter.33.cloned.1.call-done = f32[512,1024]{1,0:T(8,128)} async-done(((f32[4096,1024]{1,0:T(8,128)}), f32[512,1024]{1,0:T(8,128)}) %reduce-scatter.33.cloned.1.call-update) | async-done | bytes 2097168 | tf_op jit(solution)/shard_map/reduce_scatter | solution.py:315
  1070.2 117.8 %reduce-scatter.35.cloned.1.call-done = f32[512,1024]{1,0:T(8,128)} async-done(((f32[4096,1024]{1,0:T(8,128)}), f32[512,1024]{1,0:T(8,128)}) %reduce-scatter.35.cloned.1.call-update) | async-done | bytes 2097168 | tf_op jit(solution)/shard_map/reduce_scatter | solution.py:315
  1191.2 116.3 %reduce-scatter.31.cloned.1.call-done = f32[128,4096]{1,0:T(8,128)} async-done(((f32[1024,4096]{1,0:T(8,128)}), f32[128,4096]{1,0:T(8,128)}) %reduce-scatter.31.cloned.1.call-update) | async-done | bytes 2097168 | tf_op jit(solution)/shard_map/reduce_scatter | solution.py:313
  1309.2 117.7 %reduce-scatter.29.cloned.1.call-done = f32[128,4096]{1,0:T(8,128)} async-done(((f32[1024,4096]{1,0:T(8,128)}), f32[128,4096]{1,0:T(8,128)}) %reduce-scatter.29.cloned.1.call-update) | async-done | bytes 2097168 | tf_op jit(solution)/shard_map/reduce_scatter | solution.py:313
  1439.6 25.0 %all-reduce.18 = (bf16[1024]{0:T(1024)(128)(2,1)S(1)}, bf16[1024]{0:T(1024)(128)(2,1)S(1)}, bf16[1024]{0:T(1024)(128)(2,1)S(1)}, bf16[1024]{0:T(1024)(128)(2,1)S...) all-reduce(f32[1024]{0:T(1024)S(1)} %copy-done.94, ...), channel_id=33, replica_groups=mesh['rep'=4,'shard'=8] {'shard'}, use_global_device_ids=true, to_apply=%region_25.0.clone | all-reduce | flops 24576 | bytes 147456
  1466.1 12.7 all-reduce.19
  1485.1 171.0 %all-reduce.23.cloned.1.call-done = (bf16[2,128,1024]{2,1,0:T(8,128)(2,1)}, bf16[2,128,1024]{2,1,0:T(8,128)(2,1)}, bf16[2,128,1024]{2,1,0:T(8,128)(2,1)}, bf16[2...) async-done(((bf16[2,128,1024]{2,1,0:T(8,128)(2,1)}, bf16[2,128,1024]{2,1,0:T(8,128)(2,1)}, bf16[2,128,1024]{2,1,0:T(8,128)(2,1)}, ...) | async-done | bytes 6291472 | tf_op jit(solution)/shard_map/psum | solution.py:376
  (561 shorter events, 412.7 us)
Async XLA Ops:
  7.2 175.3 %all-gather.45.cloned.1.call-start = ((), (), s32[]{:S(2)}) async-start(), calls=%async_computation.25 | async-start | bytes 2359296 | tf_op jit(solution)/shard_map/all_gather | solution.py:263
  9.2 176.7 %all-gather.47.cloned.1.call-start = ((), (), s32[]{:S(2)}) async-start(), calls=%async_computation.26 | async-start | bytes 2359296 | tf_op jit(solution)/shard_map/all_gather | solution.py:265
  11.1 178.5 %all-gather.43.cloned.1.call-start = ((), (), s32[]{:S(2)}) async-start(), calls=%async_computation.24 | async-start | bytes 2359296 | tf_op jit(solution)/shard_map/all_gather | solution.py:266
  12.0 183.5 %all-gather.49.cloned.1.call-start = ((), (), s32[]{:S(2)}) async-start(), calls=%async_computation.27 | async-start | bytes 2359296 | tf_op jit(solution)/shard_map/all_gather | solution.py:268
  13.0 185.6 %all-gather.51.cloned.1.call-start = ((), (), s32[]{:S(2)}) async-start(), calls=%async_computation.28 | async-start | bytes 9437184 | tf_op jit(solution)/shard_map/all_gather | solution.py:272
  16.1 228.5 %all-gather.53.cloned.1.call-start = ((), (), s32[]{:S(2)}) async-start(), calls=%async_computation.29 | async-start | bytes 9437184 | tf_op jit(solution)/shard_map/all_gather | solution.py:274
  19.3 255.7 %all-gather.57.cloned.1.call-start = ((), (), s32[]{:S(2)}) async-start(), calls=%async_computation.31 | async-start | bytes 2359296 | tf_op jit(solution)/shard_map/all_gather | solution.py:263
  20.1 284.7 %all-gather.59.cloned.1.call-start = ((), (), s32[]{:S(2)}) async-start(), calls=%async_computation.32 | async-start | bytes 2359296 | tf_op jit(solution)/shard_map/all_gather | solution.py:265
  20.8 314.4 %all-gather.55.cloned.1.call-start = ((), (), s32[]{:S(2)}) async-start(), calls=%async_computation.30 | async-start | bytes 2359296 | tf_op jit(solution)/shard_map/all_gather | solution.py:266
  21.6 343.3 %all-gather.61.cloned.1.call-start = ((), (), s32[]{:S(2)}) async-start(), calls=%async_computation.33 | async-start | bytes 2359296 | tf_op jit(solution)/shard_map/all_gather | solution.py:268
  22.2 399.6 %all-gather.63.cloned.1.call-start = ((), (), s32[]{:S(2)}) async-start(), calls=%async_computation.34 | async-start | bytes 9437184 | tf_op jit(solution)/shard_map/all_gather | solution.py:272
  22.9 455.6 %all-gather.65.cloned.1.call-start = ((), (), s32[]{:S(2)}) async-start(), calls=%async_computation.35 | async-start | bytes 9437184 | tf_op jit(solution)/shard_map/all_gather | solution.py:274
  23.5 625.7 %reduce-scatter.27.cloned.1.call-start = ((), (), s32[]{:S(2)}) async-start(), calls=%async_computation.19 | async-start | bytes 4718592 | tf_op jit(solution)/shard_map/reduce_scatter | solution.py:309
  512.6 137.6 %reduce-scatter.25.cloned.1.call-start = ((), (), s32[]{:S(2)}) async-start(), calls=%async_computation.18 | async-start | bytes 4718592 | tf_op jit(solution)/shard_map/reduce_scatter | solution.py:309
  557.6 171.1 %reduce-scatter.21.cloned.1.call-start = ((), (), s32[]{:S(2)}) async-start(), calls=%async_computation.16 | async-start | bytes 4718592 | tf_op jit(solution)/shard_map/reduce_scatter | solution.py:307
  578.0 205.2 %reduce-scatter.19.cloned.1.call-start = ((), (), s32[]{:S(2)}) async-start(), calls=%async_computation.15 | async-start | bytes 4718592 | tf_op jit(solution)/shard_map/reduce_scatter | solution.py:306
  582.0 256.1 %reduce-scatter.17.cloned.1.call-start = ((), (), s32[]{:S(2)}) async-start(), calls=%async_computation.14 | async-start | bytes 4718592 | tf_op jit(solution)/shard_map/reduce_scatter | solution.py:306
  591.3 302.1 %reduce-scatter.15.cloned.1.call-start = ((), (), s32[]{:S(2)}) async-start(), calls=%async_computation.13 | async-start | bytes 4718592 | tf_op jit(solution)/shard_map/reduce_scatter | solution.py:304
  596.2 352.7 %reduce-scatter.13.cloned.1.call-start = ((), (), s32[]{:S(2)}) async-start(), calls=%async_computation.12 | async-start | bytes 4718592 | tf_op jit(solution)/shard_map/reduce_scatter | solution.py:304
  604.9 463.5 %reduce-scatter.33.cloned.1.call-start = ((), (), s32[]{:S(2)}) async-start(), calls=%async_computation.22 | async-start | bytes 18874368 | tf_op jit(solution)/shard_map/reduce_scatter | solution.py:315
  616.2 571.8 %reduce-scatter.35.cloned.1.call-start = ((), (), s32[]{:S(2)}) async-start(), calls=%async_computation.23 | async-start | bytes 18874368 | tf_op jit(solution)/shard_map/reduce_scatter | solution.py:315
  627.5 680.1 %reduce-scatter.31.cloned.1.call-start = ((), (), s32[]{:S(2)}) async-start(), calls=%async_computation.21 | async-start | bytes 18874368 | tf_op jit(solution)/shard_map/reduce_scatter | solution.py:313
  639.0 788.0 %reduce-scatter.29.cloned.1.call-start = ((), (), s32[]{:S(2)}) async-start(), calls=%async_computation.20 | async-start | bytes 18874368 | tf_op jit(solution)/shard_map/reduce_scatter | solution.py:313
  649.1 1007.0 %all-reduce.23.cloned.1.call-start = ((), (), s32[]{:S(2)}) async-start(), calls=%async_computation.36 | async-start | bytes 12582912 | tf_op jit(solution)/shard_map/psum | solution.py:376
  (136 other events, 3310.6 us)
Sparse Core Ops, SparseCore 0:
  10.5 30.5 all-gather.44
  43.0 27.8 all-gather.46
  73.4 27.8 all-gather.42
  103.1 27.9 all-gather.48
  133.4 54.4 all-gather.50
  190.2 54.3 all-gather.52
  247.1 27.8 all-gather.56
  276.9 27.8 all-gather.58
  337.0 27.8 all-gather.60
  367.4 54.3 all-gather.62
  424.1 54.3 all-gather.64
  512.8 51.3 reduce-scatter.26
  567.8 51.3 reduce-scatter.24
  622.3 51.3 reduce-scatter.22
  677.3 51.3 reduce-scatter.20
  731.8 51.2 reduce-scatter.18
  786.7 51.3 reduce-scatter.16
  842.1 51.3 reduce-scatter.14
  897.6 51.2 reduce-scatter.12
  952.5 115.9 reduce-scatter.32
  1072.0 115.9 reduce-scatter.34
  1191.6 115.9 reduce-scatter.30
  1310.9 115.9 reduce-scatter.28
  1430.9 225.0 all-reduce.22
  (1 shorter events, 27.8 us)
where the time goes:
time: 1680 us; the launch traced here: 1670 us
  waiting for transfers between devices  1170 us (70%)
  blocking collectives  189 us (11%)
  matrix products  170 us (10%)
  local copies, waits for them, and re-layouts  69 us (4%)
  other arithmetic  58.1 us (3%)
  between operations  17.3 us (1%)
    reduce_scatter x2, waiting for transfers between devices, owner_part(): lax.psum_scatter(grads[13], 'shard', scatter_dimension=0, tiled=True)  235 us
    reduce_scatter x2, waiting for transfers between devices, owner_part(): lax.psum_scatter(grads[11], 'shard', scatter_dimension=0, tiled=True)  234 us
    psum x1, waiting for transfers between devices, shards(): lax.psum(stacked[2].astype(jnp.bfloat16), 'rep').astype(jnp.float32)  171 us
    reduce_scatter x2, waiting for transfers between devices, owner_part(): lax.psum_scatter(grads[2], 'shard', scatter_dimension=0, tiled=True)  108 us
    reduce_scatter x2, waiting for transfers between devices, owner_part(): lax.psum_scatter(grads[4], 'shard', scatter_dimension=0, tiled=True)  107 us
    all_gather x2, waiting for transfers between devices, fetch_forward(): lax.all_gather(parts[13], 'shard', axis=0, tiled=True)  88.4 us
    reduce_scatter x2, waiting for transfers between devices, owner_part(): lax.psum_scatter(grads[5], 'shard', scatter_dimension=0, tiled=True)  75.3 us
    dot_general x12, matrix products, product_left(): lax.dot_general(left, right, (((0,), (0,)), ((), ())), preferred_element_...  67.6 us
  transfers between devices with their start and end apart: 25, of which 18 were waited for; matrix products, arithmetic and copies ran while one was open for 14% of the time, Pallas kernels for 0%

commit v1 on v0

v1 whole, which is shorter than its diff:
```python
import functools

import jax
import jax.numpy as jnp
from jax import lax
from jax.experimental import pallas as pl
from jax.experimental.pallas import tpu as pltpu
from jax.sharding import PartitionSpec as P

HEADS = 16
HEAD_DIM = 64
LAYERS = 2
LANES = 128
EPSILON = 1e-05
FACTOR = HEAD_DIM ** (-0.5)
F32 = jnp.float32
BF16 = jnp.bfloat16


def dot(left, right):
    return lax.dot_general(left, right, (((1,), (0,)), ((), ())), preferred_element_type=F32)


def dot_left(left, right):
    return lax.dot_general(left, right, (((0,), (0,)), ((), ())), preferred_element_type=F32)


def dot_right(left, right):
    return lax.dot_general(left, right, (((1,), (1,)), ((), ())), preferred_element_type=F32)


LIMIT = 12


def call(name, body, outs, args, flops, limit=LIMIT, scratch=()):
    moved = sum(a.size * a.dtype.itemsize for a in args)
    moved += sum(o.size * o.dtype.itemsize for o in outs)
    spec = pl.BlockSpec(memory_space=pltpu.VMEM)
    return pl.pallas_call(
        body,
        out_shape=outs,
        in_specs=[spec] * len(args),
        out_specs=[spec] * len(outs),
        scratch_shapes=scratch,
        name=name,
        compiler_params=pltpu.CompilerParams(vmem_limit_bytes=limit << 20),
        cost_estimate=pl.CostEstimate(flops=int(flops), bytes_accessed=int(moved), transcendentals=0),
    )(*args)


def shape(rows, columns, kind):
    return jax.ShapeDtypeStruct((rows, columns), kind)


def head_masks(length):
    lane = lax.broadcasted_iota(jnp.int32, (length, LANES), 1)
    count = LANES // HEAD_DIM
    return [
        ((lane >= h * HEAD_DIM) & (lane < (h + 1) * HEAD_DIM)).astype(F32).astype(BF16)
        for h in range(count)
    ]


def softmax_of(queries, keys):
    scores = dot_right(queries, keys) * FACTOR
    raised = jnp.exp(scores - jnp.max(scores, axis=-1, keepdims=True))
    return raised / jnp.sum(raised, axis=-1, keepdims=True)


def attend(queries, keys, values, masks):
    mixed = None
    for mask in masks:
        probs = softmax_of(queries * mask, keys).astype(BF16)
        part = dot(probs, values * mask)
        mixed = part if mixed is None else mixed + part
    return mixed.astype(BF16)


def attend_back(queries, keys, values, upstream, masks):
    back_q = back_k = back_v = None
    for mask in masks:
        query_h = queries * mask
        upstream_h = upstream * mask
        probs = softmax_of(query_h, keys)
        back_probs = dot_right(upstream_h, values)
        delta = jnp.sum(probs * back_probs, axis=-1, keepdims=True)
        back_scores = (probs * (back_probs - delta)).astype(BF16)
        part_v = dot_left(probs.astype(BF16), upstream_h)
        part_q = dot(back_scores, keys * mask)
        part_k = dot_left(back_scores, query_h)
        back_q = part_q if back_q is None else back_q + part_q
        back_k = part_k if back_k is None else back_k + part_k
        back_v = part_v if back_v is None else back_v + part_v
    return (
        (back_q * FACTOR).astype(BF16),
        (back_k * FACTOR).astype(BF16),
        back_v.astype(BF16),
    )


GROUP = 4


def attention(qkv, length, width):
    rows = qkv.shape[0]
    steps = width // (LANES * GROUP)
    spec = lambda part: pl.BlockSpec((length, LANES * GROUP), lambda i, j: (i, part * steps + j))

    def body(q_ref, k_ref, v_ref, o_ref):
        masks = head_masks(length)
        for block in range(GROUP):
            here = slice(block * LANES, (block + 1) * LANES)
            o_ref[:, here] = attend(q_ref[:, here], k_ref[:, here], v_ref[:, here], masks)

    return pl.pallas_call(
        body,
        grid=(rows // length, steps),
        out_shape=shape(rows, width, BF16),
        in_specs=[spec(0), spec(1), spec(2)],
        out_specs=spec(0),
        name="attn_fwd",
        compiler_params=pltpu.CompilerParams(vmem_limit_bytes=LIMIT << 20),
        cost_estimate=pl.CostEstimate(
            flops=4 * rows * length * width, bytes_accessed=8 * rows * width, transcendentals=0
        ),
    )(qkv, qkv, qkv)


def attention_back(qkv, upstream, length, width):
    rows = qkv.shape[0]
    steps = width // (LANES * GROUP)
    spec = lambda part: pl.BlockSpec((length, LANES * GROUP), lambda i, j: (i, part * steps + j))

    def body(q_ref, k_ref, v_ref, u_ref, dq_ref, dk_ref, dv_ref):
        masks = head_masks(length)
        for block in range(GROUP):
            here = slice(block * LANES, (block + 1) * LANES)
            dq_ref[:, here], dk_ref[:, here], dv_ref[:, here] = attend_back(
                q_ref[:, here], k_ref[:, here], v_ref[:, here], u_ref[:, here], masks
            )

    return pl.pallas_call(
        body,
        grid=(rows // length, steps),
        out_shape=[shape(rows, width, BF16)] * 3,
        in_specs=[spec(0), spec(1), spec(2), spec(0)],
        out_specs=[spec(0)] * 3,
        name="attn_bwd",
        compiler_params=pltpu.CompilerParams(vmem_limit_bytes=LIMIT << 20),
        cost_estimate=pl.CostEstimate(
            flops=10 * rows * length * width, bytes_accessed=14 * rows * width, transcendentals=0
        ),
    )(qkv, qkv, qkv, upstream)


def heads_forward(pair, wqkv, bias, wo, length):
    rows, width = pair[0].shape
    wide = wqkv.shape[1]
    third = wide // 3

    def body(a_ref, b_ref, w_ref, bias_ref, wo_ref, pa_ref, pb_ref, qkv_ref, o_ref):
        masks = head_masks(length)
        for at, (h_ref, p_ref) in enumerate(((a_ref, pa_ref), (b_ref, pb_ref))):
            base = at * rows
            qkv_ref[base : base + rows, :] = (dot(h_ref[...], w_ref[...]) + bias_ref[...]).astype(
                BF16
            )
            for image in range(rows // length):
                here = slice(base + image * length, base + (image + 1) * length)
                o_ref[here, :] = attend(
                    qkv_ref[here, 0:third],
                    qkv_ref[here, third : 2 * third],
                    qkv_ref[here, 2 * third :],
                    masks,
                )
            p_ref[...] = dot(o_ref[base : base + rows, :], wo_ref[...]).astype(BF16)

    return call(
        "heads_fwd",
        body,
        [
            shape(rows, width, BF16),
            shape(rows, width, BF16),
            shape(2 * rows, wide, BF16),
            shape(2 * rows, third, BF16),
        ],
        [pair[0], pair[1], wqkv, bias, wo],
        4 * rows * width * (wide + third),
    )


def heads_backward(pair, qkv, wqkv, wo, length):
    rows, width = pair[0].shape
    wide = wqkv.shape[1]
    third = wide // 3

    def body(a_ref, b_ref, qkv_ref, w_ref, wo_ref, pa_ref, pb_ref, d_ref):
        masks = head_masks(length)
        for at, (h_ref, p_ref) in enumerate(((a_ref, pa_ref), (b_ref, pb_ref))):
            base = at * rows
            back = dot_right(h_ref[...], wo_ref[...]).astype(BF16)
            for image in range(rows // length):
                here = slice(base + image * length, base + (image + 1) * length)
                dq, dk, dv = attend_back(
                    qkv_ref[here, 0:third],
                    qkv_ref[here, third : 2 * third],
                    qkv_ref[here, 2 * third :],
                    back[image * length : (image + 1) * length, :],
                    masks,
                )
                d_ref[here, 0:third] = dq
                d_ref[here, third : 2 * third] = dk
                d_ref[here, 2 * third :] = dv
            p_ref[...] = dot_right(d_ref[base : base + rows, :], w_ref[...]).astype(BF16)

    return call(
        "heads_bwd",
        body,
        [shape(rows, width, BF16), shape(rows, width, BF16), shape(2 * rows, wide, BF16)],
        [pair[0], pair[1], qkv, wqkv, wo],
        4 * rows * width * (wide + third),
    )


def feed_forward(pair, we, bias, wr):
    rows, width = pair[0].shape
    units = we.shape[1]

    def body(a_ref, b_ref, we_ref, bias_ref, wr_ref, pa_ref, pb_ref, u_ref, g_ref):
        for at, (h_ref, p_ref) in enumerate(((a_ref, pa_ref), (b_ref, pb_ref))):
            base = at * rows
            hidden = dot(h_ref[...], we_ref[...]) + bias_ref[...]
            u_ref[base : base + rows, :] = hidden
            active = (hidden * jax.nn.sigmoid(1.702 * hidden)).astype(BF16)
            g_ref[base : base + rows, :] = active
            p_ref[...] = dot(active, wr_ref[...]).astype(BF16)

    return call(
        "feed_fwd",
        body,
        [
            shape(rows, width, BF16),
            shape(rows, width, BF16),
            shape(2 * rows, units, F32),
            shape(2 * rows, units, BF16),
        ],
        [pair[0], pair[1], we, bias, wr],
        8 * rows * width * units,
    )


def feed_backward(pair, hidden, we, wr):
    rows, width = pair[0].shape
    units = we.shape[1]

    def body(a_ref, b_ref, u_ref, we_ref, wr_ref, pa_ref, pb_ref, d_ref):
        for at, (h_ref, p_ref) in enumerate(((a_ref, pa_ref), (b_ref, pb_ref))):
            base = at * rows
            back = dot_right(h_ref[...], wr_ref[...])
            u = u_ref[base : base + rows, :]
            sigma = jax.nn.sigmoid(1.702 * u)
            low = (back * (sigma + 1.702 * u * sigma * (1.0 - sigma))).astype(BF16)
            d_ref[base : base + rows, :] = low
            p_ref[...] = dot_right(low, we_ref[...]).astype(BF16)

    return call(
        "feed_bwd",
        body,
        [shape(rows, width, BF16), shape(rows, width, BF16), shape(2 * rows, units, BF16)],
        [pair[0], pair[1], hidden, we, wr],
        8 * rows * width * units,
    )


def joined_product(lefts, rights):
    depth = sum(left.shape[0] for left in lefts)
    high, wide = lefts[0].shape[1], rights[0].shape[1]
    step = min(high, 128)

    def body(*refs):
        left_refs, right_refs = refs[: len(lefts)], refs[len(lefts) : len(lefts) + len(rights)]
        out_ref, left_all, right_all = refs[len(lefts) + len(rights) :]
        for pieces, whole in ((left_refs, left_all), (right_refs, right_all)):
            at = 0
            for piece in pieces:
                whole[at : at + piece.shape[0], :] = piece[...]
                at += piece.shape[0]

        for first in range(0, high, step):
            here = slice(first, first + step)
            out_ref[here, :] = dot_left(left_all[:, here], right_all[...]).astype(BF16)

    return call(
        "wgrad",
        body,
        [shape(high, wide, BF16)],
        [*lefts, *rights],
        2 * depth * high * wide,
        scratch=[pltpu.VMEM((depth, high), BF16), pltpu.VMEM((depth, wide), BF16)],
    )[0]


def token_product(first, first_right, second, second_right, columns):
    rows, width = first.shape
    one, two, three = first_right.shape[1], second_right.shape[1], columns.shape[1]
    step = 128

    def body(a_ref, ar_ref, b_ref, br_ref, c_ref, out_ref):
        out_ref[:, 0:one] = dot_left(a_ref[...], ar_ref[...]).astype(BF16)
        out_ref[:, one : one + two] = dot_left(b_ref[...], br_ref[...]).astype(BF16)
        out_ref[:, one + two :] = c_ref[...].astype(BF16)

    tall = pl.BlockSpec((rows, step), lambda i: (0, i))
    fixed = lambda wide: pl.BlockSpec((rows, wide), lambda i: (0, 0))
    return pl.pallas_call(
        body,
        grid=(width // step,),
        out_shape=shape(width, one + two + three, BF16),
        in_specs=[tall, fixed(one), tall, fixed(two), pl.BlockSpec((step, three), lambda i: (i, 0))],
        out_specs=pl.BlockSpec((step, one + two + three), lambda i: (i, 0)),
        name="token_grad",
        compiler_params=pltpu.CompilerParams(vmem_limit_bytes=LIMIT << 20),
        cost_estimate=pl.CostEstimate(
            flops=2 * rows * width * (one + two),
            bytes_accessed=2 * width * (one + two + three),
            transcendentals=0,
        ),
    )(first, first_right, second, second_right, columns)


CHUNK = 32


def normal(values):
    center = values - jnp.mean(values, axis=-1, keepdims=True)
    inverse = lax.rsqrt(jnp.mean(center * center, axis=-1, keepdims=True) + EPSILON)
    return center * inverse, inverse


def norm_forward(stream, parts, vecs, offset, gain, shift):
    rows, width = stream.shape
    count = len(parts)

    def body(*refs):
        x_ref, part_refs, vec_ref = refs[0], refs[1 : 1 + count], refs[1 + count]
        out_refs = refs[2 + count :]

        @pl.loop(0, rows // CHUNK)
        def _(step):
            here = pl.ds(pl.multiple_of(step * CHUNK, CHUNK), CHUNK)
            total = x_ref[here, :].astype(F32)
            if count:
                added = part_refs[0][here, :].astype(F32)
                for ref in part_refs[1:]:
                    added = added + ref[here, :].astype(F32)
                total = total + (added + vec_ref[offset : offset + 1, :])
                out_refs[0][here, :] = total
            scaled, _ = normal(total)
            out_refs[-1][here, :] = (
                scaled * vec_ref[gain : gain + 1, :] + vec_ref[shift : shift + 1, :]
            ).astype(BF16)

    outs = [shape(rows, width, BF16)]
    if count:
        outs = [shape(rows, width, F32)] + outs
    return call("norm_fwd", body, outs, [stream, *parts, vecs], 10 * rows * width)


def norm_backward(parts, through, stream, vecs, gain, low):
    rows, width = stream.shape
    count = len(parts)

    def body(*refs):
        part_refs, c_ref, x_ref, vec_ref = refs[:count], refs[count], refs[count + 1], refs[count + 2]
        d_ref, sum_ref = refs[count + 3], refs[count + 4]
        sum_ref[...] = jnp.zeros_like(sum_ref)

        @pl.loop(0, rows // CHUNK)
        def _(step):
            here = pl.ds(pl.multiple_of(step * CHUNK, CHUNK), CHUNK)
            upstream = part_refs[0][here, :].astype(F32)
            for ref in part_refs[1:]:
                upstream = upstream + ref[here, :].astype(F32)
            scaled, inverse = normal(x_ref[here, :].astype(F32))
            slope = upstream * vec_ref[gain : gain + 1, :]
            inner = (
                slope
                - jnp.mean(slope, axis=-1, keepdims=True)
                - scaled * jnp.mean(slope * scaled, axis=-1, keepdims=True)
            )
            result = c_ref[here, :].astype(F32) + inner * inverse
            d_ref[here, :] = result
            sum_ref[0:1, :] += jnp.sum(upstream * scaled, axis=0, keepdims=True)
            sum_ref[1:2, :] += jnp.sum(upstream, axis=0, keepdims=True)
            if low:
                rounded = result.astype(BF16)
                refs[count + 5][here, :] = rounded
                sum_ref[2:3, :] += jnp.sum(rounded.astype(F32), axis=0, keepdims=True)

    outs = [shape(rows, width, F32), shape(8, width, F32)]
    if low:
        outs = outs + [shape(rows, width, BF16)]
    return call("norm_bwd", body, outs, [*parts, through, stream, vecs], 20 * rows * width)


def shards(
    size,
    stream_input,
    output_cotangent,
    image_mask,
    first_gain,
    first_shift,
    query_matrix,
    query_offset,
    key_matrix,
    value_matrix,
    value_offset,
    out_matrix,
    out_offset,
    second_gain,
    second_shift,
    expand_matrix,
    expand_offset,
    reduce_matrix,
    reduce_offset,
):
    images, length, width = stream_input.shape
    rows = images * length
    wide = width // LANES
    inner = size // wide
    outer_groups = [[t * inner + r for t in range(wide)] for r in range(inner)]
    inner_groups = [[t * inner + r for r in range(inner)] for t in range(wide)]
    me = lax.axis_index("shard")

    def swap(value, distance):
        return lax.ppermute(value, "shard", [(i, i ^ (distance * inner)) for i in range(size)])

    def share(value):
        if inner == 1:
            return value
        return lax.all_gather(value, "shard", axis=0, tiled=True, axis_index_groups=inner_groups)

    def unshare(value):
        if inner == 1:
            return value
        return lax.psum_scatter(
            value, "shard", scatter_dimension=0, tiled=True, axis_index_groups=inner_groups
        )

    def rows_to_columns(value):
        return lax.all_to_all(
            value, "shard", split_axis=1, concat_axis=0, tiled=True, axis_index_groups=outer_groups
        )

    def columns_to_rows(value):
        return lax.all_to_all(
            value, "shard", split_axis=0, concat_axis=1, tiled=True, axis_index_groups=outer_groups
        )

    def gather(block):
        even = [block] + [swap(block, k) for k in range(2, wide, 2)]
        blocks = []
        for one in even:
            blocks += [one, swap(one, 1)]
        return blocks

    def scatter(parts):
        even = []
        for k in range(0, wide, 2):
            total = parts[k].astype(F32) + swap(parts[k + 1], 1).astype(F32)
            even.append(total.astype(BF16))
        return [even[0]] + [swap(even[k // 2], k) for k in range(2, wide, 2)]

    def together(*values):
        return lax.optimization_barrier(values)

    replicas = lax.axis_size("rep")
    middle = (lax.axis_index("rep") == 1) | (lax.axis_index("rep") == 2)

    def add(one, other):
        return (one.astype(F32) + other.astype(F32)).astype(one.dtype)

    def inward(value):
        if replicas != 4:
            return lax.psum(value, "rep")
        return add(value, lax.ppermute(value, "rep", [(0, 1), (3, 2)]))

    def across(value):
        if replicas != 4:
            return value
        return add(value, lax.ppermute(value, "rep", [(1, 2), (2, 1)]))

    def outward(value):
        if replicas != 4:
            return value
        return jnp.where(middle, value, lax.ppermute(value, "rep", [(1, 0), (2, 3)]))

    def pairs(blocks):
        return [(blocks[k], blocks[k + 1]) for k in range(0, wide, 2)]

    def staged(stage, blocks, *rest):
        done = [stage(pair, *(r[i] if isinstance(r, list) else r for r in rest)) for i, pair in enumerate(pairs(blocks))]
        parts = [part for result in done for part in result[:2]]
        others = [list(kind) for kind in zip(*(result[2:] for result in done))]
        return parts, *others

    join = lambda pieces: jnp.concatenate(pieces, axis=0)

    names = (first_gain, first_shift, out_offset, second_gain, second_shift, reduce_offset)
    pieces = [vector[layer] for layer in range(LAYERS) for vector in names]
    pieces += [query_offset[1], value_offset[1]]
    count = len(pieces)
    vecs = lax.all_gather(jnp.concatenate(pieces), "shard", axis=0, tiled=False)
    vecs = vecs.reshape(size, count, -1).transpose(1, 0, 2).reshape(count, width).astype(F32)
    at = lambda layer, which: layer * len(names) + which

    heads = [share(m[0]).reshape(-1, wide, LANES) for m in (query_matrix, key_matrix, value_matrix)]
    wqkv = rows_to_columns(jnp.stack(heads, axis=2).reshape(-1, 3 * width))
    wo = share(out_matrix[0])
    zero = jnp.zeros((LANES,), BF16)
    bias_qkv = jnp.concatenate([share(query_offset[0]), zero, share(value_offset[0])])
    bias_qkv = bias_qkv.astype(F32)[None, :]
    we = [rows_to_columns(share(expand_matrix[layer])) for layer in range(LAYERS)]
    wr = [share(reduce_matrix[layer]) for layer in range(LAYERS)]
    bias_u = [share(expand_offset[layer]).astype(F32)[None, :] for layer in range(LAYERS)]
    whole = jnp.concatenate([query_matrix[1], key_matrix[1], value_matrix[1], out_matrix[1]], axis=1)
    whole = lax.all_gather(whole, "shard", axis=0, tiled=True)
    whole_qkv, whole_out = whole[:, : 3 * width], whole[:, 3 * width :]
    bias_whole = jnp.concatenate([vecs[count - 2], jnp.zeros((width,), F32), vecs[count - 1]])

    maskf = jnp.broadcast_to(image_mask.astype(F32)[:, None], (images, length)).reshape(rows, 1)
    x0 = stream_input.reshape(rows, width)
    top = output_cotangent.astype(F32).reshape(rows, width) * maskf
    dm1 = top.astype(BF16)

    (h1,) = norm_forward(x0, [], vecs, None, at(0, 0), at(0, 1))
    h1s = gather(h1)
    parts, qkv0, o0 = staged(lambda pair: heads_forward(pair, wqkv, bias_qkv, wo, length), h1s)
    x1, h2 = norm_forward(x0, scatter(parts), vecs, at(0, 2), at(0, 3), at(0, 4))
    x1, h2, we[0] = together(x1, h2, we[0])
    h2s = gather(h2)
    parts, u0, g0 = staged(lambda pair: feed_forward(pair, we[0], bias_u[0], wr[0]), h2s)
    x2, h3 = norm_forward(x1, scatter(parts), vecs, at(0, 5), at(1, 0), at(1, 1))
    x2, h3, we[1] = together(x2, h3, we[1])

    qkv1 = (dot(h3, whole_qkv) + bias_whole).astype(BF16)
    o1 = attention(qkv1, length, width)
    x3, h4 = norm_forward(x2, [dot(o1, whole_out)], vecs, at(1, 2), at(1, 3), at(1, 4))
    x3, h4, *dms = together(x3, h4, *gather(dm1))
    h4s = gather(h4)
    parts, u1, g1 = staged(lambda pair: feed_forward(pair, we[1], bias_u[1], wr[1]), h4s)

    backs, du1 = staged(lambda pair, u: feed_backward(pair, u, we[1], wr[1]), dms, u1)
    grad_reduce1 = joined_product(g1, dms)
    grad_expand1 = joined_product(h4s, du1)
    d3, sums_d3, da1 = norm_backward(scatter(backs), top, x3, vecs, at(1, 3), True)
    d3, sums_d3, da1, grad_reduce1, grad_expand1 = together(
        d3, sums_d3, da1, grad_reduce1, grad_expand1
    )
    grad_reduce1 = unshare(grad_reduce1)
    grad_expand1 = unshare(columns_to_rows(grad_expand1))
    back_o = dot_right(da1, whole_out).astype(BF16)
    dqkv1 = jnp.concatenate(attention_back(qkv1, back_o, length, width), axis=1)
    d2, sums_d2, dm0 = norm_backward([dot_right(dqkv1, whole_qkv)], d3, x2, vecs, at(1, 0), True)
    grad_reduce1 = lax.psum(grad_reduce1, "rep")
    d2, sums_d2, dm0, grad_reduce1, grad_expand1 = together(
        d2, sums_d2, dm0, grad_reduce1, grad_expand1
    )
    grad_expand1 = lax.psum(grad_expand1, "rep")

    last = scatter(parts)
    total = last[0].astype(F32)
    for piece in last[1:]:
        total = total + piece.astype(F32)
    output = ((x3 + (total + vecs[at(1, 5)])) * maskf).astype(BF16).reshape(images, length, width)

    column_sum = lambda value: jnp.sum(value.astype(F32), axis=0)[None, :]
    sums_qkv1 = column_sum(dqkv1).reshape(3, width)
    early = jnp.concatenate(
        [sums_d2[0:2], sums_qkv1, sums_d3[2:3], sums_d3[0:2], column_sum(dm1)], axis=0
    )
    early = jnp.pad(early, ((0, LANES - early.shape[0]), (0, 0))).T
    grad_whole1 = token_product(h3, dqkv1, o1, da1, early)

    *dms0, grad_whole1 = together(*gather(dm0), grad_whole1)
    grad_whole1 = lax.psum_scatter(grad_whole1, "shard", scatter_dimension=0, tiled=True)
    backs, du0 = staged(lambda pair, u: feed_backward(pair, u, we[0], wr[0]), dms0, u0)
    grad_reduce0 = joined_product(g0, dms0)
    grad_expand0 = joined_product(h2s, du0)
    d1, sums_d1, da0 = norm_backward(scatter(backs), d2, x1, vecs, at(0, 3), True)
    d1, sums_d1, da0, grad_reduce0, grad_expand0 = together(
        d1, sums_d1, da0, grad_reduce0, grad_expand0
    )
    grad_reduce0 = inward(unshare(grad_reduce0))
    grad_expand0 = unshare(columns_to_rows(grad_expand0))
    *das, grad_expand1, grad_reduce0 = together(*gather(da0), grad_expand1, grad_reduce0)
    grad_expand0 = inward(grad_expand0)
    grad_reduce0 = across(grad_reduce0)
    backs, dqkv0 = staged(lambda pair, qkv: heads_backward(pair, qkv, wqkv, wo, length), das, qkv0)
    *dqkv0, grad_expand1, grad_whole1 = together(*dqkv0, grad_expand1, grad_whole1)
    grad_whole1 = lax.psum(grad_whole1, "rep")
    *dqkv0, grad_expand0, grad_reduce0 = together(*dqkv0, grad_expand0, grad_reduce0)
    grad_qkv0 = unshare(columns_to_rows(joined_product(h1s, dqkv0))).reshape(-1, wide, 3, LANES)
    grad_out0 = inward(unshare(joined_product(o0, das)))
    grad_reduce0 = outward(grad_reduce0)
    grad_expand0 = across(grad_expand0)
    grad_qkv0, grad_expand0, grad_reduce0, grad_out0 = together(
        grad_qkv0, grad_expand0, grad_reduce0, grad_out0
    )
    third = lambda which: outward(across(inward(grad_qkv0[:, :, which, :].reshape(-1, width))))
    grad_query0, grad_key0, grad_value0 = third(0), third(1), third(2)
    grad_expand0 = outward(grad_expand0)
    grad_out0 = outward(across(grad_out0))
    d0, sums_d0 = norm_backward(scatter(backs), d1, x0, vecs, at(0, 0), False)

    lines = jnp.concatenate([sums_d0[0:2], sums_d1[2:3], sums_d1[0:2], sums_d2[2:3]])
    if inner == 1:
        lines = lines.reshape(-1, wide, LANES).transpose(1, 0, 2)
        lines = jnp.sum(lax.all_to_all(lines, "shard", split_axis=0, concat_axis=0), axis=0)
    else:
        lines = lax.psum_scatter(lines, "shard", scatter_dimension=1, tiled=True)
    own = [*column_sum(join(dqkv0)).reshape(3, LANES), column_sum(join(du0))[0], column_sum(join(du1))[0]]
    own = jnp.concatenate([unshare(value) for value in own]).reshape(-1, width // size)
    late = lax.psum(jnp.concatenate([lines, own]), "rep")

    early_part = grad_whole1[:, 4 * width :].astype(F32).T
    stack = lambda low, high: jnp.stack([low.astype(F32), high.astype(F32)])
    vector = lambda low, high: jnp.stack([late[low], early_part[high]])
    block = lambda which: grad_whole1[:, which * width : (which + 1) * width]
    return (
        output,
        d0.reshape(images, length, width),
        vector(0, 0),
        vector(1, 1),
        stack(grad_query0, block(0)),
        vector(6, 2),
        stack(grad_key0, block(1)),
        stack(grad_value0, block(2)),
        vector(8, 4),
        stack(grad_out0, block(3)),
        vector(2, 5),
        vector(3, 6),
        vector(4, 7),
        stack(grad_expand0, grad_expand1),
        jnp.stack([late[9:13].reshape(-1), late[13:17].reshape(-1)]),
        stack(grad_reduce0, grad_reduce1),
        vector(5, 8),
    )


def solution(mesh):
    tokens = P(("rep", "shard"), None, None)
    vector = P(None, "shard")
    matrix = P(None, "shard", None)
    params = (
        vector, vector, matrix, vector, matrix, matrix, vector, matrix,
        vector, vector, vector, matrix, vector, matrix, vector,
    )
    return jax.shard_map(
        functools.partial(shards, mesh.shape["shard"]),
        mesh=mesh,
        in_specs=(tokens, tokens, P(("rep", "shard"))) + params,
        out_specs=(tokens, tokens) + params,
        check_vma=False,
    )
```

time: 1680 us -> 727 us (0.43)
  waiting for transfers between devices: 1170 us -> 231 us
  matrix products: 170 us -> 14.4 us
  Pallas kernels: 0 us -> 127 us
  blocking collectives: 189 us -> 72.4 us
  starting transfers between devices: 1.4 us -> 113 us
    reduce_scatter x12 -> x1, waiting for transfers between devices: 759 us -> 0.01 us  [shards(): lax.psum_scatter(grad_whole1, 'shard', scatter_dimension=0, tiled=True)]
    all_gather x12 -> x1, waiting for transfers between devices: 235 us -> 0.01 us  [shards(): whole = lax.all_gather(whole, 'shard', axis=0, tiled=True)]
    ppermute x0 -> x102, waiting for transfers between devices: none -> 205 us  [the longest x84 184 us: swap(): lax.ppermute(value, 'shard', [(i, i ^ distance * inner) for i in range(si...]
    dot_general x48 -> x4, matrix products: 170 us -> 14.4 us  [the longest x2 7.77 us: dot_right(): lax.dot_general(left, right, (((1,), (1,)), ((), ())), preferred_element_...]
    psum x1 -> x3, waiting for transfers between devices: 171 us -> 25.8 us  [the longest x1 25.8 us: shards(): grad_reduce1 = lax.psum(grad_reduce1, 'rep')]
    all_gather x18 -> x1, blocking collectives: 151 us -> 10.7 us  [shards(): vecs = lax.all_gather(jnp.concatenate(pieces), 'shard', axis=0, tiled=False)]
    pallas_call x0 -> x41, Pallas kernels: none -> 127 us  [the longest x38 108 us: call(): pl.pallas_call(body, out_shape=outs, in_specs=[spec] * len(args), out_spe...]
    ppermute x0 -> x102, starting transfers between devices: none -> 85.2 us  [the longest x84 55.3 us: swap(): lax.ppermute(value, 'shard', [(i, i ^ distance * inner) for i in range(si...]
  transfers between devices with their start and end apart: 25 -> 114, of which waited for: 18 -> 30; matrix products, arithmetic and copies ran while one was open for 14% -> 14% of each run, Pallas kernels for 0% -> 17%
where the time goes in v1:
time: 727 us; the launch traced here: 717 us
  waiting for transfers between devices  231 us (32%)
  Pallas kernels  127 us (17%)
  starting transfers between devices  113 us (16%)
  local copies, waits for them, and re-layouts  82.4 us (11%)
  blocking collectives  72.4 us (10%)
  other arithmetic  60.1 us (8%)
  between operations  16.5 us (2%)
  matrix products  14.4 us (2%)
    ppermute x84, waiting for transfers between devices, swap(): lax.ppermute(value, 'shard', [(i, i ^ distance * inner) for i in range(si...  184 us
    pallas_call x38, Pallas kernels, call(): pl.pallas_call(body, out_shape=outs, in_specs=[spec] * len(args), out_spe...  108 us
    psum x1, blocking collectives, shards(): late = lax.psum(jnp.concatenate([lines, own]), 'rep')  61.8 us
    unnamed x368, local copies, waits for them, and re-layouts  58.4 us
    ppermute x84, starting transfers between devices, swap(): lax.ppermute(value, 'shard', [(i, i ^ distance * inner) for i in range(si...  55.3 us
    psum x1, waiting for transfers between devices, shards(): grad_reduce1 = lax.psum(grad_reduce1, 'rep')  25.8 us
    ppermute x6, waiting for transfers between devices, outward(): lax.ppermute(value, 'rep', [(1, 0), (2, 3)])  21 us
    convert_element_type x23, other arithmetic, scatter(): even.append(total.astype(BF16))  16.9 us
  transfers between devices with their start and end apart: 114, of which 30 were waited for; matrix products, arithmetic and copies ran while one was open for 14% of the time, Pallas kernels for 17%

profile of v1, /device:TPU:0, one launch (start us, length us, event | category | flops | bytes accessed | tf_op | source)
XLA Modules:
  0.0 716.6 jit_solution(7699179462843414725)
XLA Ops:
  13.9 10.7 %all-gather.1 = bf16[8,1,1792]{2,1,0:T(2,128)(2,1)S(1)} all-gather(bf16[1,1,1792]{2,1,0:T(2,128)(2,1)S(1)} %reshape.147), channel_id=2, replica_groups=mesh['rep'=4,'shard'=8] {'shard'}, dimensions={0}, use_global_device_ids=true | all-gather | bytes 32256 | tf_op jit(solution)/shard_map/all_gather | solution.py:513
  35.7 8.3 %collective-permute-done.2.a_ref.refs_2_ = bf16[192,1024]{1,0:T(8,128)(2,1)S(1)} collective-permute-done((bf16[192,1024]{1,0:T(8,128)(2,1)S(1)}, bf16[192,1024]{1,0:T(8,128)(2,1)S(1)}, u32[]{:S(2)}, u32[]{:S(2)}) %collective-permute-start.2) | collective-permute-done | bytes 393248 | tf_op jit(solution)/shard_map/ppermute | solution.py:436
  45.2 27.3 %collective-permute-done.10.a_ref.refs_6_ = bf16[192,1024]{1,0:T(8,128)(2,1)} collective-permute-done((bf16[192,1024]{1,0:T(8,128)(2,1)S(1)}, bf16[192,1024]{1,0:T(8,128)(2,1)}, u32[]{:S(2)}, u32[]{:S(2)}) %collective-permute-start.10) | collective-permute-done | bytes 393248 | tf_op jit(solution)/shard_map/ppermute | solution.py:436
  106.3 7.8 %collective-permute-done.5.refs_2_ = bf16[192,1024]{1,0:T(8,128)(2,1)S(1)} collective-permute-done((bf16[192,1024]{1,0:T(8,128)(2,1)S(1)}, bf16[192,1024]{1,0:T(8,128)(2,1)S(1)}, u32[]{:S(2)}, u32[]{:S(2)}) %collective-permute-start.5) | collective-permute-done | bytes 393248 | tf_op jit(solution)/shard_map/ppermute | solution.py:436
  114.1 9.7 %collective-permute-done.9.refs_3_ = bf16[192,1024]{1,0:T(8,128)(2,1)S(1)} collective-permute-done((bf16[192,1024]{1,0:T(8,128)(2,1)S(1)}, bf16[192,1024]{1,0:T(8,128)(2,1)S(1)}, u32[]{:S(2)}, u32[]{:S(2)}) %collective-permute-start.9) | collective-permute-done | bytes 393248 | tf_op jit(solution)/shard_map/ppermute | solution.py:436
  142.0 17.2 %collective-permute-done.24.a_ref.refs_6_ = bf16[192,1024]{1,0:T(8,128)(2,1)} collective-permute-done((bf16[192,1024]{1,0:T(8,128)(2,1)}, bf16[192,1024]{1,0:T(8,128)(2,1)}, u32[]{:S(2)}, u32[]{:S(2)}) %collective-permute-start.24) | collective-permute-done | bytes 393248 | tf_op jit(solution)/shard_map/ppermute | solution.py:436
  187.1 8.6 %collective-permute-done.19.refs_2_ = bf16[192,1024]{1,0:T(8,128)(2,1)S(1)} collective-permute-done((bf16[192,1024]{1,0:T(8,128)(2,1)S(1)}, bf16[192,1024]{1,0:T(8,128)(2,1)S(1)}, u32[]{:S(2)}, u32[]{:S(2)}) %collective-permute-start.19) | collective-permute-done | bytes 393248 | tf_op jit(solution)/shard_map/ppermute | solution.py:436
  196.1 6.9 collective-permute-done.27.refs_4_
  211.4 6.0 attn_fwd.1.b_ref
  224.9 8.6 %collective-permute-done.37.a_ref.refs_2_ = bf16[192,1024]{1,0:T(8,128)(2,1)S(1)} collective-permute-done((bf16[192,1024]{1,0:T(8,128)(2,1)S(1)}, bf16[192,1024]{1,0:T(8,128)(2,1)S(1)}, u32[]{:S(2)}, u32[]{:S(2)}) %collective-permute-start.37) | collective-permute-done | bytes 393248 | tf_op jit(solution)/shard_map/ppermute | solution.py:436
  233.5 8.1 %collective-permute-done.41.a_ref.refs_4_ = bf16[192,1024]{1,0:T(8,128)(2,1)S(1)} collective-permute-done((bf16[192,1024]{1,0:T(8,128)(2,1)S(1)}, bf16[192,1024]{1,0:T(8,128)(2,1)S(1)}, u32[]{:S(2)}, u32[]{:S(2)}) %collective-permute-start.41) | collective-permute-done | bytes 393248 | tf_op jit(solution)/shard_map/ppermute | solution.py:436
  295.3 7.0 collective-permute-done.53.refs_2_
  312.8 8.4 %attn_bwd.1 = (bf16[192,1024]{1,0:T(8,128)(2,1)S(1)}, bf16[192,1024]{1,0:T(8,128)(2,1)S(1)}, bf16[192,1024]{1,0:T(8,128)(2,1)S(1)}) custom-call(bf16[192,3072]{1,0:T(8,128)(2,1)S(1)} %fusion.7.q_ref.k_ref.v_ref, bf16[192,3072]{1,0:T(8,128)(2,1)S(1)} %fusion.7.q_ref.k_ref.v_ref, bf16[192,3072]{1,0:T(8,128)(2,1)S(1)} %fusion.7.q_ref.k_ref.v_ref, ...), custom_call_target="tpu_custom_call" | custom-call | flops 188743680 | bytes 2752512 | tf_op jit(solution)/shard_map/attn_bwd/pallas_call | solution.py:142
  321.4 5.1 fusion.refs_0_
  332.4 25.8 %all-reduce.5.cloned.1.call-done = bf16[512,1024]{1,0:T(8,128)(2,1)} async-done(((bf16[512,1024]{1,0:T(8,128)(2,1)}), bf16[512,1024]{1,0:T(8,128)(2,1)}) %all-reduce.5.cloned.1.call-update) | async-done | bytes 1048592 | tf_op jit(solution)/shard_map/psum | solution.py:565
  363.1 7.5 %collective-permute-done.57.a_ref.refs_6_ = bf16[192,1024]{1,0:T(8,128)(2,1)} collective-permute-done((bf16[192,1024]{1,0:T(8,128)(2,1)}, bf16[192,1024]{1,0:T(8,128)(2,1)}, u32[]{:S(2)}, u32[]{:S(2)}) %collective-permute-start.57) | collective-permute-done | bytes 393248 | tf_op jit(solution)/shard_map/ppermute | solution.py:436
  370.7 8.7 %collective-permute-done.59.a_ref.refs_8_ = bf16[192,1024]{1,0:T(8,128)(2,1)} collective-permute-done((bf16[192,1024]{1,0:T(8,128)(2,1)}, bf16[192,1024]{1,0:T(8,128)(2,1)}, u32[]{:S(2)}, u32[]{:S(2)}) %collective-permute-start.59) | collective-permute-done | bytes 393248 | tf_op jit(solution)/shard_map/ppermute | solution.py:436
  425.0 7.4 %collective-permute-done.67.refs_2_ = bf16[192,1024]{1,0:T(8,128)(2,1)S(1)} collective-permute-done((bf16[192,1024]{1,0:T(8,128)(2,1)S(1)}, bf16[192,1024]{1,0:T(8,128)(2,1)S(1)}, u32[]{:S(2)}, u32[]{:S(2)}) %collective-permute-start.67) | collective-permute-done | bytes 393248 | tf_op jit(solution)/shard_map/ppermute | solution.py:436
  447.1 14.1 %collective-permute-done.71.a_ref.refs_6_ = bf16[192,1024]{1,0:T(8,128)(2,1)S(1)} collective-permute-done((bf16[192,1024]{1,0:T(8,128)(2,1)S(1)}, bf16[192,1024]{1,0:T(8,128)(2,1)S(1)}, u32[]{:S(2)}, u32[]{:S(2)}) %collective-permute-start.71) | collective-permute-done | bytes 393248 | tf_op jit(solution)/shard_map/ppermute | solution.py:436
  487.2 5.2 heads_bwd.5
  503.7 7.2 %collective-permute-done.44 = bf16[192,1024]{1,0:T(8,128)(2,1)} collective-permute-done((bf16[192,1024]{1,0:T(8,128)(2,1)}, bf16[192,1024]{1,0:T(8,128)(2,1)}, u32[]{:S(2)}, u32[]{:S(2)}) %collective-permute-start.44) | collective-permute-done | bytes 393248 | tf_op jit(solution)/shard_map/ppermute | solution.py:436
  543.9 7.6 %collective-permute-done.82.refs_2_ = bf16[192,1024]{1,0:T(8,128)(2,1)S(1)} collective-permute-done((bf16[192,1024]{1,0:T(8,128)(2,1)S(1)}, bf16[192,1024]{1,0:T(8,128)(2,1)S(1)}, u32[]{:S(2)}, u32[]{:S(2)}) %collective-permute-start.82) | collective-permute-done | bytes 393248 | tf_op jit(solution)/shard_map/ppermute | solution.py:436
  578.1 61.8 %psum.30 = f32[17,128]{1,0:T(8,128)S(1)} all-reduce(f32[17,128]{1,0:T(8,128)S(1)} %pad_maximum_fusion.2), channel_id=1, replica_groups=mesh['rep'=4,'shard'=8] {'rep'}, use_global_device_ids=true, to_apply=%region_9.10 | all-reduce | flops 2176 | bytes 17408 | tf_op jit(solution)/shard_map/psum | solution.py:624
  680.6 12.3 %collective-permute-done.100 = bf16[128,1024]{1,0:T(8,128)(2,1)S(1)} collective-permute-done((bf16[128,1024]{1,0:T(8,128)(2,1)S(1)}, bf16[128,1024]{1,0:T(8,128)(2,1)S(1)}, u32[]{:S(2)}, u32[]{:S(2)}) %collective-permute-start.100) | collective-permute-done | bytes 262176 | tf_op jit(solution)/shard_map/ppermute | solution.py:496
  (750 shorter events, 402.8 us)
Async XLA Ops:
  7.2 199.9 %all-gather.4.cloned.1.call-start = ((), (), s32[]{:S(2)}) async-start(), calls=%async_computation.8 | async-start | bytes 9437184 | tf_op jit(solution)/shard_map/all_gather | solution.py:527
  29.3 43.2 %all-to-all-start = ((bf16[128,8,384]{2,0,1:T(8,128)(2,1)}), bf16[128,8,384]{2,0,1:T(8,128)(2,1)S(1)}, u32[]{:S(2)}, u32[]{:S(2)}) async-start(bf16[128,8,384]{2,0,1:T(8,128)(2,1)} %copy.74), calls=%async_computation | async-start | bytes 1572864 | tf_op jit(solution)/shard_map/all_to_all | solution.py:451
  32.9 39.6 %collective-permute-start.10 = (bf16[192,1024]{1,0:T(8,128)(2,1)S(1)}, bf16[192,1024]{1,0:T(8,128)(2,1)}, u32[]{:S(2)}, u32[]{:S(2)}) collective-permute-start(bf16[192,1024]{1,0:T(8,128)(2,1)S(1)} %norm_fwd.4.a_ref.refs_0_), channel_id=1, source_target_pairs={{0,6},{1,7},{2,4},{3,5},{4,2},{5,3},{6,0},{7,1},{8,14},{9,15},{10,... | collective-permute-start | bytes 1179656 | tf_op jit(solution)/shard_map/ppermute | solution.py:436
  44.6 33.8 %collective-permute-start.7 = (bf16[192,1024]{1,0:T(8,128)(2,1)S(1)}, bf16[192,1024]{1,0:T(8,128)(2,1)}, u32[]{:S(2)}, u32[]{:S(2)}) collective-permute-start(bf16[192,1024]{1,0:T(8,128)(2,1)S(1)} %collective-permute-done.6.a_ref.refs_4_), channel_id=1, source_target_pairs={{0,1},{1,0},{2,3},{3,2},{4,5},{5,4},{6,7},{7,6},{8,9},{9,8},{10,11... | collective-permute-start | bytes 1179656 | tf_op jit(solution)/shard_map/ppermute | solution.py:436
  44.6 46.2 %collective-permute-start = (bf16[192,1024]{1,0:T(8,128)(2,1)S(1)}, bf16[192,1024]{1,0:T(8,128)(2,1)}, u32[]{:S(2)}, u32[]{:S(2)}) collective-permute-start(bf16[192,1024]{1,0:T(8,128)(2,1)S(1)} %norm_fwd.4.a_ref.refs_0_), channel_id=1, source_target_pairs={{0,1},{1,0},{2,3},{3,2},{4,5},{5,4},{6,7},{7,6},{8,9},{9,8},{10,11... | collective-permute-start | bytes 1179656 | tf_op jit(solution)/shard_map/ppermute | solution.py:436
  87.0 39.7 %all-to-all-start.1 = ((bf16[128,8,512]{2,0,1:T(8,128)(2,1)}), bf16[128,8,512]{2,0,1:T(8,128)(2,1)S(1)}, u32[]{:S(2)}, u32[]{:S(2)}) async-start(bf16[128,8,512]{2,0,1:T(8,128)(2,1)} %copy.75), calls=%async_computation.1 | async-start | bytes 2097152 | tf_op jit(solution)/shard_map/all_to_all | solution.py:451
  131.7 74.4 %all-to-all-start.2 = ((bf16[128,8,512]{2,0,1:T(8,128)(2,1)}), bf16[128,8,512]{2,0,1:T(8,128)(2,1)S(1)}, u32[]{:S(2)}, u32[]{:S(2)}) async-start(bf16[128,8,512]{2,0,1:T(8,128)(2,1)} %copy.76), calls=%async_computation.2 | async-start | bytes 2097152 | tf_op jit(solution)/shard_map/all_to_all | solution.py:451
  135.3 223.0 %all-reduce.5.cloned.1.call-start = ((), (), s32[]{:S(2)}) async-start(), calls=%async_computation.9 | async-start | bytes 2097152 | tf_op jit(solution)/shard_map/psum | solution.py:565
  185.2 36.1 %collective-permute-start.28 = (bf16[192,1024]{1,0:T(8,128)(2,1)}, bf16[192,1024]{1,0:T(8,128)(2,1)}, u32[]{:S(2)}, u32[]{:S(2)}) collective-permute-start(bf16[192,1024]{1,0:T(8,128)(2,1)} %get-tuple-element.225.a_ref.refs_4_), channel_id=1, source_target_pairs={{0,1},{1,0},{2,3},{3,2},{4,5},{5,4},{6,7},{7,6},{8,9},{9,8},{10,11... | collective-permute-start | bytes 1179656 | tf_op jit(solution)/shard_map/ppermute | solution.py:436
  187.0 34.3 %collective-permute-start.30 = (bf16[192,1024]{1,0:T(8,128)(2,1)}, bf16[192,1024]{1,0:T(8,128)(2,1)}, u32[]{:S(2)}, u32[]{:S(2)}) collective-permute-start(bf16[192,1024]{1,0:T(8,128)(2,1)} %collective-permute-done.29.a_ref.refs_6_), channel_id=1, source_target_pairs={{0,1},{1,0},{2,3},{3,2},{4,5},{5,4},{6,7},{7,6},{8,9},{9,8},{10,11... | collective-permute-start | bytes 1179656 | tf_op jit(solution)/shard_map/ppermute | solution.py:436
  249.9 44.2 %collective-permute-start.49 = (bf16[192,1024]{1,0:T(8,128)(2,1)}, bf16[192,1024]{1,0:T(8,128)(2,1)}, u32[]{:S(2)}, u32[]{:S(2)}) collective-permute-start(bf16[192,1024]{1,0:T(8,128)(2,1)} %get-tuple-element.229), channel_id=1, source_target_pairs={{0,1},{1,0},{2,3},{3,2},{4,5},{5,4},{6,7},{7,6},{8,9},{9,8},{10,11... | collective-permute-start | bytes 1179656 | tf_op jit(solution)/shard_map/ppermute | solution.py:436
  310.2 176.1 %all-reduce.7.cloned.1.call-start = ((), (), s32[]{:S(2)}) async-start(), calls=%async_computation.10 | async-start | bytes 2097152 | tf_op jit(solution)/shard_map/psum | solution.py:569
  358.3 206.1 %reduce-scatter.2.cloned.1.call-start = ((), (), s32[]{:S(2)}) async-start(), calls=%async_computation.11 | async-start | bytes 9732096 | tf_op jit(solution)/shard_map/reduce_scatter | solution.py:586
  398.4 43.6 %collective-permute-start.47 = (bf16[192,1024]{1,0:T(8,128)(2,1)S(1)}, bf16[192,1024]{1,0:T(8,128)(2,1)S(1)}, u32[]{:S(2)}, u32[]{:S(2)}) collective-permute-start(bf16[192,1024]{1,0:T(8,128)(2,1)S(1)} %copy-done.121), channel_id=1, source_target_pairs={{0,1},{1,0},{2,3},{3,2},{4,5},{5,4},{6,7},{7,6},{8,9},{9,8},{10,11... | collective-permute-start | bytes 1179656 | tf_op jit(solution)/shard_map/ppermute | solution.py:436
  436.5 45.3 %collective-permute-start.77 = (bf16[512,1024]{1,0:T(8,128)(2,1)}, bf16[512,1024]{1,0:T(8,128)(2,1)}, u32[]{:S(2)}, u32[]{:S(2)}) collective-permute-start(bf16[512,1024]{1,0:T(8,128)(2,1)} %wgrad.8), channel_id=1, source_target_pairs={{0,8},{24,16},{1,9},{25,17},{2,10},{26,18},{3,11},{27,19},{4,12},{... | collective-permute-start | bytes 3145736 | tf_op jit(solution)/shard_map/ppermute | solution.py:486
  446.1 32.2 %collective-permute-start.75 = (bf16[192,1024]{1,0:T(8,128)(2,1)S(1)}, bf16[192,1024]{1,0:T(8,128)(2,1)S(1)}, u32[]{:S(2)}, u32[]{:S(2)}) collective-permute-start(bf16[192,1024]{1,0:T(8,128)(2,1)S(1)} %get-tuple-element.304.a_ref.refs_4_), channel_id=1, source_target_pairs={{0,6},{1,7},{2,4},{3,5},{4,2},{5,3},{6,0},{7,1},{8,14},{9,15},{10,... | collective-permute-start | bytes 1179656 | tf_op jit(solution)/shard_map/ppermute | solution.py:436
  466.4 47.6 %all-to-all-start.5 = ((bf16[8,128,512]{2,1,0:T(8,128)(2,1)}), bf16[8,128,512]{2,1,0:T(8,128)(2,1)}, u32[]{:S(2)}, u32[]{:S(2)}) async-start(bf16[8,128,512]{2,1,0:T(8,128)(2,1)} %bitcast.209), calls=%async_computation.6 | async-start | bytes 2097152 | tf_op jit(solution)/shard_map/all_to_all | solution.py:456
  493.2 35.6 %collective-permute-start.79 = (bf16[192,1024]{1,0:T(8,128)(2,1)}, bf16[192,1024]{1,0:T(8,128)(2,1)}, u32[]{:S(2)}, u32[]{:S(2)}) collective-permute-start(bf16[192,1024]{1,0:T(8,128)(2,1)} %get-tuple-element.313), channel_id=1, source_target_pairs={{0,1},{1,0},{2,3},{3,2},{4,5},{5,4},{6,7},{7,6},{8,9},{9,8},{10,11... | collective-permute-start | bytes 1179656 | tf_op jit(solution)/shard_map/ppermute | solution.py:436
  516.3 42.1 %collective-permute-start.85 = (bf16[128,4096]{1,0:T(8,128)(2,1)}, bf16[128,4096]{1,0:T(8,128)(2,1)}, u32[]{:S(2)}, u32[]{:S(2)}) collective-permute-start(bf16[128,4096]{1,0:T(8,128)(2,1)} %bitcast.73), channel_id=1, source_target_pairs={{0,8},{24,16},{1,9},{25,17},{2,10},{26,18},{3,11},{27,19},{4,12},{... | collective-permute-start | bytes 3145736 | tf_op jit(solution)/shard_map/ppermute | solution.py:486
  558.1 100.3 %all-reduce.9.cloned.1.call-start = ((), (), s32[]{:S(2)}) async-start(), calls=%async_computation.12 | async-start | bytes 2162688 | tf_op jit(solution)/shard_map/psum | solution.py:601
  564.3 77.8 %collective-permute-start.87 = (bf16[128,4096]{1,0:T(8,128)(2,1)}, bf16[128,4096]{1,0:T(8,128)(2,1)}, u32[]{:S(2)}, u32[]{:S(2)}) collective-permute-start(bf16[128,4096]{1,0:T(8,128)(2,1)} %add_convert_fusion.2), channel_id=1, source_target_pairs={{8,16},{16,8},{9,17},{17,9},{10,18},{18,10},{11,19},{19,11},{12,20... | collective-permute-start | bytes 3145736 | tf_op jit(solution)/shard_map/ppermute | solution.py:491
  572.2 68.3 %all-to-all-start.6 = ((bf16[8,128,384]{2,1,0:T(8,128)(2,1)}), bf16[8,128,384]{2,1,0:T(8,128)(2,1)}, u32[]{:S(2)}, u32[]{:S(2)}) async-start(bf16[8,128,384]{2,1,0:T(8,128)(2,1)} %bitcast.49), calls=%async_computation.7 | async-start | bytes 1572864 | tf_op jit(solution)/shard_map/all_to_all | solution.py:456
  576.5 67.1 %collective-permute-start.88 = (bf16[512,1024]{1,0:T(8,128)(2,1)}, bf16[512,1024]{1,0:T(8,128)(2,1)}, u32[]{:S(2)}, u32[]{:S(2)}) collective-permute-start(bf16[512,1024]{1,0:T(8,128)(2,1)} %add_convert_fusion.1), channel_id=1, source_target_pairs={{8,0},{16,24},{9,1},{17,25},{10,2},{18,26},{11,3},{19,27},{12,4},{... | collective-permute-start | bytes 3145736 | tf_op jit(solution)/shard_map/ppermute | solution.py:496
  654.8 51.2 %collective-permute-start.101 = (bf16[128,4096]{1,0:T(8,128)(2,1)S(1)}, bf16[128,4096]{1,0:T(8,128)(2,1)}, u32[]{:S(2)}, u32[]{:S(2)}) collective-permute-start(bf16[128,4096]{1,0:T(8,128)(2,1)S(1)} %add_convert_fusion), channel_id=1, source_target_pairs={{8,0},{16,24},{9,1},{17,25},{10,2},{18,26},{11,3},{19,27},{12,4},{... | collective-permute-start | bytes 3145736 | tf_op jit(solution)/shard_map/ppermute | solution.py:496
  (261 other events, 2814.4 us)
Sparse Core Ops, SparseCore 0:
  10.9 75.2 all-gather.3
  306.0 52.1 all-reduce.4
  361.3 51.1 all-reduce.6
  415.9 111.1 reduce-scatter.1
  567.9 66.5 all-reduce.8
